TPU v7x, 512 devices: a whole 4x4x16 slice. The times are simulated.
512 devices in a mesh: seq: 64 (over y, z), req: 8 (over x, core).
Axes of the slice: x: 4, y: 4, z: 16, core: 2. Of those that a mesh axis runs over, the one named last changes fastest.
Arguments:
- new_token_queries: bfloat16 [4, 64, 2048], P(None, 'req'), may hold values from -48 to 48
- new_token_keys: bfloat16 [4, 64, 1024], P(None, 'req'), may hold values from -48 to 48
- new_token_values: bfloat16 [4, 64, 1024], P(None, 'req'), may hold values from -6 to 6
- key_cache: bfloat16 [64, 2048, 1024], P('req', 'seq'), may hold values from -48 to 48
- value_cache: bfloat16 [64, 2048, 1024], P('req', 'seq'), may hold values from -6 to 6
- cache_len: int32 [64], P('req'), may hold values from 1 to 2048, 34816 in all
- resid: bfloat16 [4, 64, 2048], P(None, 'req'), may hold values from -6 to 6
- gain: bfloat16 [2048], replicated, may hold values from 0.5 to 1.5
- w_gate: bfloat16 [2048, 6144], P('seq', 'req'), may hold values from -0.125 to 0.125
- w_up: bfloat16 [2048, 6144], P('seq', 'req'), may hold values from -0.125 to 0.125
- w_down: bfloat16 [6144, 2048], P('req', 'seq'), may hold values from -0.078125 to 0.078125
Outputs:
- out: bfloat16 [4, 64, 2048], P(None, 'req')
All inputs are finite; a program needn't handle non-finite values. No bound on the sum of `cache_len` on one device may be relied on, other than what follows from the above.
Results may differ from a plain program's by a relative error of at most 0.006.
Values may be sent and summed in bfloat16 or wider, within the bound.
A program may use at most 128 MiB of HBM per device.

v0:
```python
import math
import jax
import jax.numpy as jnp
from jax import lax
from jax.sharding import PartitionSpec as P

QUERY_HEADS = 16
KEY_VALUE_HEADS = 8
HEAD_SIZE = 128
NEG_FILL = -1e30
EPSILON = 1e-06


def partial_softmax(q, keys, values, valid):
    scores = jnp.einsum("rkmd,rbkd->rkmb", q, keys, preferred_element_type=jnp.float32) / math.sqrt(
        HEAD_SIZE
    )
    inside = valid[:, None]
    scores = jnp.where(inside, scores, NEG_FILL)
    highest = jnp.max(scores, axis=-1)
    weights = jnp.where(inside, jnp.exp(scores - highest[..., None]), 0.0).astype(jnp.bfloat16)
    totals = jnp.sum(weights.astype(jnp.float32), axis=-1)
    weighted = jnp.einsum("rkmb,rbkd->rkmd", weights, values, preferred_element_type=jnp.float32)
    return (highest, totals, weighted)


def body(q, nk, nv, kc, vc, cache_len, resid, gain, w_gate, w_up, w_down):
    steps, rows, model = q.shape
    page = kc.shape[1]
    width = w_gate.shape[0]
    units = w_gate.shape[1]
    group = QUERY_HEADS // KEY_VALUE_HEADS
    me = lax.axis_index("seq")
    positions = me * page + jnp.arange(page, dtype=jnp.int32)
    valid = (positions[None, :] < cache_len[:, None])[:, None, :]
    qv = q.reshape(steps, rows, KEY_VALUE_HEADS, group, HEAD_SIZE).transpose(1, 2, 0, 3, 4)
    qv = qv.reshape(rows, KEY_VALUE_HEADS, steps * group, HEAD_SIZE)
    keys = kc.reshape(rows, page, KEY_VALUE_HEADS, HEAD_SIZE)
    values = vc.reshape(rows, page, KEY_VALUE_HEADS, HEAD_SIZE)
    local = partial_softmax(qv, keys, values, jnp.broadcast_to(valid, (rows, steps * group, page)))
    highest = lax.pmax(local[0], "seq")
    factor = jnp.exp(local[0] - highest)
    totals, weighted = lax.psum((factor * local[1], factor[..., None] * local[2]), "seq")
    fk = jnp.swapaxes(nk, 0, 1).reshape(rows, steps, KEY_VALUE_HEADS, HEAD_SIZE)
    fv = jnp.swapaxes(nv, 0, 1).reshape(rows, steps, KEY_VALUE_HEADS, HEAD_SIZE)
    step_of = jnp.arange(steps * group, dtype=jnp.int32) // group
    causal = jnp.arange(steps, dtype=jnp.int32)[None, :] <= step_of[:, None]
    fresh = partial_softmax(
        qv, fk, fv, jnp.broadcast_to(causal[None], (rows, steps * group, steps))
    )
    peak = jnp.maximum(highest, fresh[0])
    a = jnp.exp(highest - peak)
    b = jnp.exp(fresh[0] - peak)
    total = a * totals + b * fresh[1]
    acc = a[..., None] * weighted + b[..., None] * fresh[2]
    attn = (acc / total[..., None]).astype(jnp.bfloat16)
    attn = attn.reshape(rows, KEY_VALUE_HEADS, steps, group, HEAD_SIZE).transpose(2, 0, 1, 3, 4)
    attn = attn.reshape(steps, rows, model)
    attn = lax.optimization_barrier(attn).astype(jnp.float32)
    stream = (resid.astype(jnp.float32) + attn).astype(jnp.bfloat16)
    stream = lax.optimization_barrier(stream).astype(jnp.float32)
    scaled = lax.rsqrt(jnp.mean(stream * stream, axis=-1, keepdims=True) + EPSILON)
    normed = (stream * scaled * gain.astype(jnp.float32)).astype(jnp.bfloat16)
    own = lax.dynamic_slice_in_dim(normed, me * width, width, 2)
    every = lax.all_gather(own, "req", axis=1, tiled=True).reshape(-1, width)
    joined = jnp.concatenate([w_gate, w_up], axis=1)
    sums = lax.psum(jnp.dot(every, joined, preferred_element_type=jnp.float32), "seq")
    hidden = (jax.nn.silu(sums[:, :units]) * sums[:, units:]).astype(jnp.bfloat16)
    down = jnp.dot(hidden, w_down, preferred_element_type=jnp.float32)
    down = lax.psum_scatter(down.reshape(steps, -1, width), "req", scatter_dimension=1, tiled=True)
    piece = (lax.dynamic_slice_in_dim(stream, me * width, width, 2) + down).astype(jnp.bfloat16)
    return lax.all_gather(piece, "seq", axis=2, tiled=True)


def solution(mesh):
    placed = (
        P(None, "req", None),
        P(None, "req", None),
        P(None, "req", None),
        P("req", "seq", None),
        P("req", "seq", None),
        P("req"),
        P(None, "req", None),
        P(),
        P("seq", "req"),
        P("seq", "req"),
        P("req", "seq"),
    )
    return jax.shard_map(
        body, mesh=mesh, in_specs=placed, out_specs=P(None, "req", None), check_vma=False
    )
```

profile of v0, /device:TPU:8, one launch (start us, length us, event | category | flops | bytes accessed | tf_op | source)
XLA Modules:
  0.0 988.8 jit_solution(13132273959055247014)
XLA Ops:
  6.6 1.1 copy.49
  7.6 0.7 broadcast_compare_fusion
  8.4 1.5 fusion.27
  9.9 261.8 %pmax.7 = f32[8,8,8]{2,1,0:T(8,128)S(1)} all-reduce(f32[8,8,8]{2,1,0:T(8,128)S(1)} %get-tuple-element.10), channel_id=1, replica_groups=mesh['seq'=64,'req'=8] {'seq'}, use_global_device_ids=true, to_apply=%region_1.2 | all-reduce | flops 512 | bytes 4096 | tf_op jit(solution)/shard_map/pmax | solution.py:41
  271.6 0.3 convert_reduce_fusion
  271.9 1.0 convolution_multiply_fusion.1
  273.1 0.2 fusion.28
  273.3 0.1 convert_reduce_fusion.1
  273.4 0.8 dynamic-slice.2
  274.2 274.0 %psum.22 = f32[8,8,8]{2,1,0:T(8,128)S(1)} all-reduce(f32[8,8,8]{2,1,0:T(8,128)S(1)} %get-tuple-element.8), channel_id=1, replica_groups=mesh['seq'=64,'req'=8] {'seq'}, use_global_device_ids=true, to_apply=%region_5.6 | all-reduce | flops 512 | bytes 4096 | tf_op jit(solution)/shard_map/psum | solution.py:43
  548.3 1.4 fusion.3
  549.7 0.2 copy.54
  549.9 0.1 multiply_reduce_fusion
  550.2 13.1 %all_gather.6 = bf16[4,64,32]{2,0,1:T(4,128)(2,1)S(1)} all-gather(bf16[4,8,32]{2,0,1:T(4,128)(2,1)S(1)} %copy.55), channel_id=1, replica_groups=mesh['seq'=64,'req'=8] {'req'}, dimensions={1}, use_global_device_ids=true | all-gather | bytes 18432 | tf_op jit(solution)/shard_map/all_gather | solution.py:65
  563.5 1.5 fusion.12
  565.0 1.3 dynamic-slice
  566.9 286.0 %all-reduce.6.cloned.1.call-done = f32[256,1536]{1,0:T(8,128)} async-done(((f32[256,1536]{1,0:T(8,128)}), f32[256,1536]{1,0:T(8,128)}) %all-reduce.6.cloned.1.call-update) | async-done | bytes 1572880 | tf_op jit(solution)/shard_map/psum | solution.py:67
  852.9 1.7 fusion.10
  854.6 0.1 reshape.72
  854.7 0.1 copy.57
  854.9 24.7 %all-reduce = f32[4,64,32]{2,0,1:T(4,128)S(1)} all-reduce(f32[4,64,32]{2,0,1:T(4,128)S(1)} %copy.57), channel_id=2, replica_groups=mesh['seq'=64,'req'=8] {'req'}, use_global_device_ids=true, to_apply=%region_9.10.clone | all-reduce | flops 8192 | bytes 65536
  879.7 0.1 copy.59
  879.8 100.1 %all_gather.7 = bf16[4,8,2048]{1,0,2:T(4,128)(2,1)S(1)} all-gather(bf16[4,8,32]{1,0,2:T(4,128)(2,1)S(1)} %copy.59), channel_id=1, replica_groups=mesh['seq'=64,'req'=8] {'seq'}, dimensions={2}, use_global_device_ids=true | all-gather | bytes 133120 | tf_op jit(solution)/shard_map/all_gather | solution.py:72
  979.9 2.1 copy.60
  (33 shorter events, 0.6 us)
Async XLA Ops:
  6.5 265.4 %copy-start = (bf16[8,32,1024]{2,1,0:T(8,128)(2,1)S(1)}, bf16[8,32,1024]{2,1,0:T(8,128)(2,1)}, u32[]{:S(2)}) copy-start(bf16[8,32,1024]{2,1,0:T(8,128)(2,1)} %param.15) | copy-start | bytes 1572868
  6.5 541.8 %all-reduce.4.cloned.1.call-start = ((), (), s32[]{:S(2)}) async-start(), calls=%async_computation | async-start | bytes 524288 | tf_op jit(solution)/shard_map/psum | solution.py:43
  6.5 266.5 %copy-start.4 = (bf16[4,8,1024]{2,1,0:T(8,128)(2,1)S(1)}, bf16[4,8,1024]{2,1,0:T(8,128)(2,1)}, u32[]{:S(2)}) copy-start(bf16[4,8,1024]{2,1,0:T(8,128)(2,1)} %param.12) | copy-start | bytes 196612
  9.8 538.5 %copy-start.5 = (bf16[4,8,1024]{2,1,0:T(8,128)(2,1)S(1)}, bf16[4,8,1024]{2,1,0:T(8,128)(2,1)}, u32[]{:S(2)}) copy-start(bf16[4,8,1024]{2,1,0:T(8,128)(2,1)} %param.13) | copy-start | bytes 196612
  273.0 579.9 %all-reduce.6.cloned.1.call-start = ((), (), s32[]{:S(2)}) async-start(), calls=%async_computation.1 | async-start | bytes 3145728 | tf_op jit(solution)/shard_map/psum | solution.py:67
  273.1 276.8 %copy-start.1 = (bf16[4,8,2048]{2,1,0:T(8,128)(2,1)S(1)}, bf16[4,8,2048]{2,1,0:T(8,128)(2,1)}, u32[]{:S(2)}) copy-start(bf16[4,8,2048]{2,1,0:T(8,128)(2,1)} %param.17) | copy-start | bytes 393220
  548.3 15.1 %copy-start.2 = (bf16[32,768]{1,0:T(8,128)(2,1)S(1)}, bf16[32,768]{1,0:T(8,128)(2,1)}, u32[]{:S(2)}) copy-start(bf16[32,768]{1,0:T(8,128)(2,1)} %param.20) | copy-start | bytes 147460
  548.3 15.1 %copy-start.3 = (bf16[32,768]{1,0:T(8,128)(2,1)S(1)}, bf16[32,768]{1,0:T(8,128)(2,1)}, u32[]{:S(2)}) copy-start(bf16[32,768]{1,0:T(8,128)(2,1)} %param.19) | copy-start | bytes 147460
  563.4 289.5 %copy-start.6 = (bf16[768,32]{0,1:T(8,128)(2,1)S(1)}, bf16[768,32]{0,1:T(8,128)(2,1)}, u32[]{:S(2)}) copy-start(bf16[768,32]{0,1:T(8,128)(2,1)} %param.21) | copy-start | bytes 147460
Sparse Core Ops, SparseCore 0:
  273.1 274.0 all-reduce.3
  565.1 287.7 all-reduce.5
where the time goes:
time: 989 us
  blocking collectives  674 us (68%)
  waiting for transfers between devices  286 us (29%)
  between operations  14.3 us (1%)
    psum x1, waiting for transfers between devices, body(): lax.psum(jnp.dot(every, joined, preferred_element_type=jnp.float32), 'seq')  286 us
    psum x1, blocking collectives, body(): lax.psum((factor * local[1], factor[..., None] * local[2]), 'seq')  274 us
    pmax x1, blocking collectives, body(): highest = lax.pmax(local[0], 'seq')  262 us
    all_gather x1, blocking collectives, body(): return lax.all_gather(piece, 'seq', axis=2, tiled=True)  100 us
    unnamed x1, blocking collectives  24.7 us
  transfers between devices with their start and end apart: 2, of which 1 were waited for; matrix products, arithmetic and copies ran while one was open for 0% of the time, Pallas kernels for 0%

commit v1 on v0

--- a/solution.py
+++ b/solution.py
@@ -64,7 +64,9 @@
     own = lax.dynamic_slice_in_dim(normed, me * width, width, 2)
     every = lax.all_gather(own, "req", axis=1, tiled=True).reshape(-1, width)
     joined = jnp.concatenate([w_gate, w_up], axis=1)
-    sums = lax.psum(jnp.dot(every, joined, preferred_element_type=jnp.float32), "seq")
+    sums = jnp.sum(
+        lax.all_gather(jnp.dot(every, joined, preferred_element_type=jnp.float32), "seq"), axis=0
+    )
     hidden = (jax.nn.silu(sums[:, :units]) * sums[:, units:]).astype(jnp.bfloat16)
     down = jnp.dot(hidden, w_down, preferred_element_type=jnp.float32)
     down = lax.psum_scatter(down.reshape(steps, -1, width), "req", scatter_dimension=1, tiled=True)

time: 989 us -> 1490 us (1.51)
  waiting for transfers between devices: 286 us -> 756 us
  other arithmetic: 1.51 us -> 32.3 us
    all_gather x0 -> x1, waiting for transfers between devices: none -> 756 us  [body(): lax.all_gather(jnp.dot(every, joined, preferred_element_type=jnp.float32)...]
    psum x1 -> x0, waiting for transfers between devices: 286 us -> none  [body(): lax.psum(jnp.dot(every, joined, preferred_element_type=jnp.float32), 'seq')]
    reduce_sum x0 -> x1, other arithmetic: none -> 30.8 us  [body(): jnp.sum(lax.all_gather(jnp.dot(every, joined, preferred_element_type=jnp....]
where the time goes in v1:
time: 1490 us
  waiting for transfers between devices  756 us (51%)
  blocking collectives  676 us (45%)
  other arithmetic  32.3 us (2%)
    all_gather x1, waiting for transfers between devices, body(): lax.all_gather(jnp.dot(every, joined, preferred_element_type=jnp.float32)...  756 us
    psum x1, blocking collectives, body(): lax.psum((factor * local[1], factor[..., None] * local[2]), 'seq')  274 us
    pmax x1, blocking collectives, body(): highest = lax.pmax(local[0], 'seq')  262 us
    all_gather x1, blocking collectives, body(): return lax.all_gather(piece, 'seq', axis=2, tiled=True)  101 us
    reduce_sum x1, other arithmetic, body(): jnp.sum(lax.all_gather(jnp.dot(every, joined, preferred_element_type=jnp....  30.8 us
  transfers between devices with their start and end apart: 2, of which 1 were waited for; matrix products, arithmetic and copies ran while one was open for 0% of the time, Pallas kernels for 0%

profile of v1, /device:TPU:8, one launch (start us, length us, event | category | flops | bytes accessed | tf_op | source)
XLA Modules:
  0.0 1490.0 jit_solution(15799828115258735750)
XLA Ops:
  6.6 1.1 copy.49
  7.6 0.7 broadcast_compare_fusion
  8.4 1.5 fusion.27
  9.9 261.8 %pmax.7 = f32[8,8,8]{2,1,0:T(8,128)S(1)} all-reduce(f32[8,8,8]{2,1,0:T(8,128)S(1)} %get-tuple-element.10), channel_id=1, replica_groups=mesh['seq'=64,'req'=8] {'seq'}, use_global_device_ids=true, to_apply=%region_1.2 | all-reduce | flops 512 | bytes 4096 | tf_op jit(solution)/shard_map/pmax | solution.py:41
  271.6 0.3 convert_reduce_fusion
  271.9 1.0 convolution_multiply_fusion.1
  273.1 0.2 fusion.28
  273.3 0.1 convert_reduce_fusion.1
  273.4 0.8 dynamic-slice.2
  274.2 274.1 %psum.15 = f32[8,8,8]{2,1,0:T(8,128)S(1)} all-reduce(f32[8,8,8]{2,1,0:T(8,128)S(1)} %get-tuple-element.8), channel_id=1, replica_groups=mesh['seq'=64,'req'=8] {'seq'}, use_global_device_ids=true, to_apply=%region_5.6 | all-reduce | flops 512 | bytes 4096 | tf_op jit(solution)/shard_map/psum | solution.py:43
  548.4 1.3 fusion.3
  549.7 0.2 copy.54
  550.0 0.1 multiply_reduce_fusion
  550.2 13.0 all_gather.12
  563.4 1.5 fusion.12
  565.0 1.3 dynamic-slice
  566.9 755.6 %all-gather.3.cloned.1.call-done = f32[16384,1536]{1,0:T(8,128)} async-done(((f32[256,1536]{1,0:T(8,128)}), f32[16384,1536]{1,0:T(8,128)}) %all-gather.3.cloned.1.call-update) | async-done | bytes 100663312 | tf_op jit(solution)/shard_map/all_gather | solution.py:68
  1322.5 30.8 %reduce_sum.39 = f32[256,1536]{1,0:T(8,128)S(1)} reduce(f32[64,256,1536]{2,1,0:T(8,128)} %bitcast.10, f32[]{:T(128)} %constant.41.clone.1), dimensions={0}, to_apply=%region_8.9 | reduce | flops 24772608 | bytes 102236160 | tf_op jit(solution)/shard_map/reduce_sum | solution.py:67
  1353.3 0.3 fusion.10
  1353.6 0.1 reshape.72
  1353.8 0.1 copy.57
  1353.9 26.4 %all-reduce = f32[4,64,32]{2,0,1:T(4,128)S(1)} all-reduce(f32[4,64,32]{2,0,1:T(4,128)S(1)} %copy.57), channel_id=3, replica_groups=mesh['seq'=64,'req'=8] {'req'}, use_global_device_ids=true, to_apply=%region_9.10.clone | all-reduce | flops 8192 | bytes 65536
  1380.5 100.6 %all_gather.15 = bf16[4,8,2048]{1,0,2:T(4,128)(2,1)S(1)} all-gather(bf16[4,8,32]{1,0,2:T(4,128)(2,1)S(1)} %copy.59), channel_id=1, replica_groups=mesh['seq'=64,'req'=8] {'seq'}, dimensions={2}, use_global_device_ids=true | all-gather | bytes 133120 | tf_op jit(solution)/shard_map/all_gather | solution.py:74
  1481.1 2.1 copy.60
  (34 shorter events, 0.7 us)
Async XLA Ops:
  6.5 265.4 %copy-start = (bf16[8,32,1024]{2,1,0:T(8,128)(2,1)S(1)}, bf16[8,32,1024]{2,1,0:T(8,128)(2,1)}, u32[]{:S(2)}) copy-start(bf16[8,32,1024]{2,1,0:T(8,128)(2,1)} %param.15) | copy-start | bytes 1572868
  6.5 541.8 %all-reduce.3.cloned.1.call-start = ((), (), s32[]{:S(2)}) async-start(), calls=%async_computation | async-start | bytes 524288 | tf_op jit(solution)/shard_map/psum | solution.py:43
  6.5 266.5 %copy-start.4 = (bf16[4,8,1024]{2,1,0:T(8,128)(2,1)S(1)}, bf16[4,8,1024]{2,1,0:T(8,128)(2,1)}, u32[]{:S(2)}) copy-start(bf16[4,8,1024]{2,1,0:T(8,128)(2,1)} %param.12) | copy-start | bytes 196612
  9.8 538.5 %copy-start.5 = (bf16[4,8,1024]{2,1,0:T(8,128)(2,1)S(1)}, bf16[4,8,1024]{2,1,0:T(8,128)(2,1)}, u32[]{:S(2)}) copy-start(bf16[4,8,1024]{2,1,0:T(8,128)(2,1)} %param.13) | copy-start | bytes 196612
  273.0 1049.6 %all-gather.3.cloned.1.call-start = ((), (), s32[]{:S(2)}) async-start(), calls=%async_computation.1 | async-start | bytes 102236160 | tf_op jit(solution)/shard_map/all_gather | solution.py:68
  273.1 276.8 %copy-start.1 = (bf16[4,8,2048]{2,1,0:T(8,128)(2,1)S(1)}, bf16[4,8,2048]{2,1,0:T(8,128)(2,1)}, u32[]{:S(2)}) copy-start(bf16[4,8,2048]{2,1,0:T(8,128)(2,1)} %param.17) | copy-start | bytes 393220
  548.3 15.1 %copy-start.2 = (bf16[32,768]{1,0:T(8,128)(2,1)S(1)}, bf16[32,768]{1,0:T(8,128)(2,1)}, u32[]{:S(2)}) copy-start(bf16[32,768]{1,0:T(8,128)(2,1)} %param.20) | copy-start | bytes 147460
  548.4 15.1 %copy-start.3 = (bf16[32,768]{1,0:T(8,128)(2,1)S(1)}, bf16[32,768]{1,0:T(8,128)(2,1)}, u32[]{:S(2)}) copy-start(bf16[32,768]{1,0:T(8,128)(2,1)} %param.19) | copy-start | bytes 147460
  1322.5 30.8 %copy-start.6 = (bf16[768,32]{0,1:T(8,128)(2,1)S(1)}, bf16[768,32]{0,1:T(8,128)(2,1)}, u32[]{:S(2)}) copy-start(bf16[768,32]{0,1:T(8,128)(2,1)} %param.21) | copy-start | bytes 147460
Sparse Core Ops, SparseCore 0:
  273.1 274.0 all-reduce.2
  565.1 757.3 all-gather.2

commit v2 on v0

--- a/solution.py
+++ b/solution.py
@@ -69,7 +69,9 @@
     down = jnp.dot(hidden, w_down, preferred_element_type=jnp.float32)
     down = lax.psum_scatter(down.reshape(steps, -1, width), "req", scatter_dimension=1, tiled=True)
     piece = (lax.dynamic_slice_in_dim(stream, me * width, width, 2) + down).astype(jnp.bfloat16)
-    return lax.all_gather(piece, "seq", axis=2, tiled=True)
+    return jnp.concatenate(
+        lax.all_to_all(jnp.stack([piece] * lax.axis_size("seq")), "seq", 0, 0), axis=2
+    )
 
 
 def solution(mesh):

time: 989 us -> 928 us (0.938)
  blocking collectives: 674 us -> 577 us
  waiting for transfers between devices: 286 us -> 322 us
    all_gather x1 -> x0, blocking collectives: 100 us -> none  [body(): return lax.all_gather(piece, 'seq', axis=2, tiled=True)]
    reduce_scatter x0 -> x1, waiting for transfers between devices: none -> 34.6 us  [body(): lax.psum_scatter(down.reshape(steps, -1, width), 'req', scatter_dimension...]
    all_to_all x0 -> x1, blocking collectives: none -> 29.8 us  [body(): lax.all_to_all(jnp.stack([piece] * lax.axis_size('seq')), 'seq', 0, 0)]
    unnamed x1 -> x0, blocking collectives: 24.7 us -> none
  transfers between devices with their start and end apart: 2 -> 3, of which waited for: 1 -> 2; matrix products, arithmetic and copies ran while one was open for 0% -> 0% of each run, Pallas kernels for 0% -> 0%
where the time goes in v2:
time: 928 us; the launch traced here: 927 us
  blocking collectives  577 us (62%)
  waiting for transfers between devices  322 us (35%)
  between operations  13.3 us (1%)
    psum x1, waiting for transfers between devices, body(): lax.psum(jnp.dot(every, joined, preferred_element_type=jnp.float32), 'seq')  288 us
    psum x1, blocking collectives, body(): lax.psum((factor * local[1], factor[..., None] * local[2]), 'seq')  274 us
    pmax x1, blocking collectives, body(): highest = lax.pmax(local[0], 'seq')  262 us
    reduce_scatter x1, waiting for transfers between devices, body(): lax.psum_scatter(down.reshape(steps, -1, width), 'req', scatter_dimension...  34.6 us
    all_to_all x1, blocking collectives, body(): lax.all_to_all(jnp.stack([piece] * lax.axis_size('seq')), 'seq', 0, 0)  29.8 us
  transfers between devices with their start and end apart: 3, of which 2 were waited for; matrix products, arithmetic and copies ran while one was open for 0% of the time, Pallas kernels for 0%

profile of v2, /device:TPU:8, one launch (start us, length us, event | category | flops | bytes accessed | tf_op | source)
XLA Modules:
  0.0 927.4 jit_solution(8359449445522266432)
XLA Ops:
  6.6 1.1 copy.26
  7.6 0.7 broadcast_compare_fusion
  8.4 1.5 fusion.26
  9.9 261.8 %pmax.7 = f32[8,8,8]{2,1,0:T(8,128)S(1)} all-reduce(f32[8,8,8]{2,1,0:T(8,128)S(1)} %get-tuple-element.10), channel_id=1, replica_groups=mesh['seq'=64,'req'=8] {'seq'}, use_global_device_ids=true, to_apply=%region_1.2 | all-reduce | flops 512 | bytes 4096 | tf_op jit(solution)/shard_map/pmax | solution.py:41
  271.6 0.3 convert_reduce_fusion
  271.9 1.0 convolution_multiply_fusion.1
  273.1 0.2 fusion.27
  273.3 0.1 convert_reduce_fusion.1
  273.4 0.8 dynamic-slice
  274.2 274.0 %psum.22 = f32[8,8,8]{2,1,0:T(8,128)S(1)} all-reduce(f32[8,8,8]{2,1,0:T(8,128)S(1)} %get-tuple-element.8), channel_id=1, replica_groups=mesh['seq'=64,'req'=8] {'seq'}, use_global_device_ids=true, to_apply=%region_5.6 | all-reduce | flops 512 | bytes 4096 | tf_op jit(solution)/shard_map/psum | solution.py:43
  548.3 1.4 fusion.3
  549.7 0.2 copy.31
  549.9 0.1 multiply_reduce_fusion
  550.1 11.8 %all_gather.3 = bf16[4,64,32]{2,1,0:T(8,128)(2,1)S(1)} all-gather(bf16[4,8,32]{2,1,0:T(8,128)(2,1)S(1)} %multiply_convert_fusion), channel_id=1, replica_groups=mesh['seq'=64,'req'=8] {'req'}, dimensions={1}, use_global_device_ids=true | all-gather | bytes 18432 | tf_op jit(solution)/shard_map/all_gather | solution.py:65
  561.9 1.5 fusion.12
  563.5 287.5 %all-reduce.5.cloned.1.call-done = f32[256,1536]{1,0:T(8,128)} async-done(((f32[256,1536]{1,0:T(8,128)}), f32[256,1536]{1,0:T(8,128)}) %all-reduce.5.cloned.1.call-update) | async-done | bytes 1572880 | tf_op jit(solution)/shard_map/psum | solution.py:67
  851.0 2.4 fusion.10
  853.4 34.6 %reduce-scatter.2.cloned.1.call-done = f32[4,8,32]{2,1,0:T(8,128)} async-done(((f32[4,64,32]{2,1,0:T(8,128)}), f32[4,8,32]{2,1,0:T(8,128)}) %reduce-scatter.2.cloned.1.call-update) | async-done | bytes 4112 | tf_op jit(solution)/shard_map/reduce_scatter | solution.py:70
  888.0 0.8 add_convert_fusion.1
  888.9 0.4 reshape.83
  889.3 29.8 %all_to_all.5 = bf16[64,2,512]{2,1,0:T(2,128)(2,1)S(1)} all-to-all(bf16[64,2,512]{2,1,0:T(2,128)(2,1)S(1)} %reshape.83), channel_id=1, replica_groups=mesh['seq'=64,'req'=8] {'seq'}, dimensions={0} | all-to-all | bytes 262144 | tf_op jit(solution)/shard_map/all_to_all | solution.py:73
  919.1 0.3 reshape.84
  919.4 0.2 copy.33
  919.7 1.2 reshape.82
  (31 shorter events, 0.5 us)
Async XLA Ops:
  6.5 265.4 %copy-start = (bf16[8,32,1024]{2,1,0:T(8,128)(2,1)S(1)}, bf16[8,32,1024]{2,1,0:T(8,128)(2,1)}, u32[]{:S(2)}) copy-start(bf16[8,32,1024]{2,1,0:T(8,128)(2,1)} %param.15) | copy-start | bytes 1572868
  6.5 541.8 %all-reduce.3.cloned.1.call-start = ((), (), s32[]{:S(2)}) async-start(), calls=%async_computation.2 | async-start | bytes 524288 | tf_op jit(solution)/shard_map/psum | solution.py:43
  6.5 266.5 %copy-start.4 = (bf16[4,8,1024]{2,1,0:T(8,128)(2,1)S(1)}, bf16[4,8,1024]{2,1,0:T(8,128)(2,1)}, u32[]{:S(2)}) copy-start(bf16[4,8,1024]{2,1,0:T(8,128)(2,1)} %param.12) | copy-start | bytes 196612
  9.8 538.5 %copy-start.5 = (bf16[4,8,1024]{2,1,0:T(8,128)(2,1)S(1)}, bf16[4,8,1024]{2,1,0:T(8,128)(2,1)}, u32[]{:S(2)}) copy-start(bf16[4,8,1024]{2,1,0:T(8,128)(2,1)} %param.13) | copy-start | bytes 196612
  273.0 578.0 %all-reduce.5.cloned.1.call-start = ((), (), s32[]{:S(2)}) async-start(), calls=%async_computation.3 | async-start | bytes 3145728 | tf_op jit(solution)/shard_map/psum | solution.py:67
  273.1 276.8 %copy-start.1 = (bf16[4,8,2048]{2,1,0:T(8,128)(2,1)S(1)}, bf16[4,8,2048]{2,1,0:T(8,128)(2,1)}, u32[]{:S(2)}) copy-start(bf16[4,8,2048]{2,1,0:T(8,128)(2,1)} %param.17) | copy-start | bytes 393220
  548.3 13.6 %copy-start.2 = (bf16[32,768]{1,0:T(8,128)(2,1)S(1)}, bf16[32,768]{1,0:T(8,128)(2,1)}, u32[]{:S(2)}) copy-start(bf16[32,768]{1,0:T(8,128)(2,1)} %param.20) | copy-start | bytes 147460
  548.3 13.6 %copy-start.3 = (bf16[32,768]{1,0:T(8,128)(2,1)S(1)}, bf16[32,768]{1,0:T(8,128)(2,1)}, u32[]{:S(2)}) copy-start(bf16[32,768]{1,0:T(8,128)(2,1)} %param.19) | copy-start | bytes 147460
  561.9 289.1 %copy-start.6 = (bf16[768,32]{0,1:T(8,128)(2,1)S(1)}, bf16[768,32]{0,1:T(8,128)(2,1)}, u32[]{:S(2)}) copy-start(bf16[768,32]{0,1:T(8,128)(2,1)} %param.21) | copy-start | bytes 147460
  563.5 324.6 %reduce-scatter.2.cloned.1.call-start = ((), (), s32[]{:S(2)}) async-start(), calls=%async_computation.4 | async-start | bytes 147456 | tf_op jit(solution)/shard_map/reduce_scatter | solution.py:70
Sparse Core Ops, SparseCore 0:
  273.1 274.0 all-reduce.2
  563.6 287.3 all-reduce.4
  854.0 33.9 reduce-scatter.1
